TPU v7x, 256 devices: a whole 4x4x8 slice. The times are simulated.
256 devices in a mesh: depth: 32 (over z, x_hi, core), shot: 8 (over y, x_lo).
Axes of the slice: x: 4 (x_hi: 2, x_lo: 2; x = x_hi * 2 + x_lo), y: 4, z: 8, core: 2. Of those that a mesh axis runs over, the one named last changes fastest.
Arguments:
- courant: float32 [512, 64, 128], P('depth'), may hold values from 0.04 to 0.2
- wave_before: float32 [8, 512, 64, 128], P('shot', 'depth'), may hold values from -10 to 10
- wave_current: float32 [8, 512, 64, 128], P('shot', 'depth'), may hold values from -10 to 10
- adjoint_after: float32 [8, 512, 64, 128], P('shot', 'depth'), may hold values from -10 to 10
- adjoint_current: float32 [8, 512, 64, 128], P('shot', 'depth'), may hold values from -10 to 10
- source_cell: int32 [8], P('shot'), may hold values from 0 to 4194303
- wavelet: float32 [8, 4], P('shot'), may hold values from -15 to 15
- receiver_cell: int32 [8, 256], P('shot'), may hold values from 0 to 4194303
- residual: float32 [8, 4, 256], P('shot'), may hold values from -12 to 12
- history: float32 [2, 5, 512, 64, 128], P(None, None, 'depth', 'shot'), may hold values from -23 to 23, as said below
Outputs:
- gradient: float32 [512, 64, 128], P('depth', 'shot')
- direction: float32 [512, 64, 128], P('depth', 'shot')
- courant_next: float32 [512, 64, 128], P('depth')
Inputs may be any that keep to these rules, and one draw needn't show every extreme that they name: In every pair the sum over all cells of history[0] times history[1] is positive.
All inputs are finite; a program needn't handle non-finite values.
Results may differ from a plain program's by a relative error of at most 0.00026.
Values sent between devices are 32-bit elements; how exact they have to be, the bound alone decides.
A program may use at most 128 MiB of HBM per device.

v0:
```python
import jax
import jax.numpy as jnp
from jax import lax
from jax.sharding import PartitionSpec as P

STEPS = 4
PAIRS = 5
coefficients = (-205.0 / 72.0, 8.0 / 5.0, -1.0 / 5.0, 8.0 / 315.0, -1.0 / 560.0)


def with_halo(cells, sides, width):
    for axis, dim in sides:
        count = lax.axis_size(axis)
        ends = count - 1
        head = lax.slice_in_dim(cells, 0, width, axis=dim)
        tail = lax.slice_in_dim(cells, cells.shape[dim] - width, cells.shape[dim], axis=dim)
        cells = jnp.concatenate(
            [
                lax.ppermute(tail, axis, [(i, (i + 1) % count) for i in range(ends)]),
                cells,
                lax.ppermute(head, axis, [((i + 1) % count, i) for i in range(ends)]),
            ],
            axis=dim,
        )
    return cells


def laplace_core(extended):
    interior = extended[4:-4]
    count_rows = interior.shape[0]
    width_x = interior.shape[1]
    width_y = interior.shape[2]
    padded = jnp.pad(interior, ((0, 0), (4, 4), (4, 4)))
    summed = 3.0 * coefficients[0] * interior
    for reach in range(1, 5):
        weight = coefficients[reach]
        summed = summed + weight * (
            extended[4 + reach : 4 + reach + count_rows]
            + extended[4 - reach : 4 - reach + count_rows]
        )
        summed = summed + weight * (
            padded[:, 4 + reach : 4 + reach + width_x, 4 : 4 + width_y]
            + padded[:, 4 - reach : 4 - reach + width_x, 4 : 4 + width_y]
        )
        summed = summed + weight * (
            padded[:, 4 : 4 + width_x, 4 + reach : 4 + reach + width_y]
            + padded[:, 4 : 4 + width_x, 4 - reach : 4 - reach + width_y]
        )
    return summed


def inject(volume, cell_ids, values, offset):
    count_rows = volume.shape[0]
    plane_size = volume.shape[1] * volume.shape[2]
    depth_row = cell_ids // plane_size - offset
    remainder = cell_ids % plane_size
    inside = (depth_row >= 0) & (depth_row < count_rows)
    row_safe = jnp.clip(depth_row, 0, count_rows - 1)
    return volume.at[row_safe, remainder // volume.shape[2], remainder % volume.shape[2]].add(
        jnp.where(inside, values, jnp.zeros_like(values))
    )


def per_device(
    courant,
    wave_before,
    wave_current,
    adjoint_after,
    adjoint_current,
    source_cell,
    wavelet,
    receiver_cell,
    residual,
    history,
):
    slab_rows = courant.shape[0]
    first_row = lax.axis_index("depth") * slab_rows
    shot_count = lax.axis_size("shot")
    summed = jnp.zeros(courant.shape, jnp.float32)
    laplacians = []
    wave_old = wave_before[0]
    wave_now = wave_current[0]
    for moment in range(STEPS):
        extended = with_halo(wave_now, (("depth", 0),), 4)
        laplacian = laplace_core(extended)
        wave_new = 2.0 * wave_now - wave_old + courant * laplacian
        wave_new = inject(wave_new, source_cell, wavelet[0, moment : moment + 1], first_row)
        laplacians.append(laplacian)
        wave_old, wave_now = (wave_now, wave_new)
    adjoint_old = adjoint_after[0]
    adjoint_now = adjoint_current[0]
    for moment in reversed(range(STEPS)):
        extended = with_halo(courant * adjoint_now, (("depth", 0),), 4)
        adjoint_new = 2.0 * adjoint_now - adjoint_old + laplace_core(extended)
        adjoint_new = inject(adjoint_new, receiver_cell[0], residual[0, moment], first_row)
        summed = summed + adjoint_new * laplacians[moment]
        adjoint_old, adjoint_now = (adjoint_now, adjoint_new)
    grad_piece = lax.psum_scatter(summed, "shot", scatter_dimension=1, tiled=True) * (
        1.0 / (shot_count * STEPS)
    )
    displaced = history[0]
    changes = history[1]
    pair_dots = jnp.sum(displaced * changes, axis=(1, 2, 3))
    last_square = jnp.sum(changes[PAIRS - 1] * changes[PAIRS - 1])
    curvature, last_square = lax.psum((pair_dots, last_square), ("depth", "shot"))
    inverse = 1.0 / curvature
    search = grad_piece
    alphas = [None] * PAIRS
    for number in reversed(range(PAIRS)):
        alphas[number] = inverse[number] * lax.psum(
            jnp.sum(displaced[number] * search), ("depth", "shot")
        )
        search = search - alphas[number] * changes[number]
    scaled = curvature[PAIRS - 1] / last_square * search
    for number in range(PAIRS):
        correction = inverse[number] * lax.psum(
            jnp.sum(changes[number] * scaled), ("depth", "shot")
        )
        scaled = scaled + (alphas[number] - correction) * displaced[number]
    direction = -scaled
    piece_width = grad_piece.shape[1]
    own_courant = lax.dynamic_slice_in_dim(
        courant, lax.axis_index("shot") * piece_width, piece_width, 1
    )
    next_piece = own_courant + 0.05 * direction
    courant_next = lax.all_gather(next_piece, "shot", axis=1, tiled=True)
    return (grad_piece, direction, courant_next)


def solution(mesh):
    return jax.shard_map(
        per_device,
        mesh=mesh,
        in_specs=(
            P("depth", None, None),
            P("shot", "depth", None, None),
            P("shot", "depth", None, None),
            P("shot", "depth", None, None),
            P("shot", "depth", None, None),
            P("shot"),
            P("shot", None),
            P("shot", None),
            P("shot", None, None),
            P(None, None, "depth", "shot", None),
        ),
        out_specs=(P("depth", "shot", None), P("depth", "shot", None), P("depth", None, None)),
        check_vma=False,
    )
```

profile of v0, /device:TPU:32, one launch (start us, length us, event | category | flops | bytes accessed | tf_op | source)
XLA Modules:
  0.0 1052.4 jit_solution(10083528813388528675)
XLA Ops:
  8.9 3.9 collective-permute-start.2
  16.2 6.2 collective-permute-start
  33.0 23.9 %scatter_fusion = f32[16,64,128]{2,1,0:T(8,128)S(1)} fusion(f32[16,64,128]{2,1,0:T(8,128)S(1)} %fusion.184, s32[256]{0:T(256)S(1)} %bitcast.166, f32[256]{0:T(256)} %get-tuple-element.95), kind=kCustom, calls=%fused_computation | custom fusion | flops 256 | bytes 6144 | tf_op jit(solution)/shard_map/scatter-add | solution.py:59
  57.0 3.7 fusion.344
  61.3 4.0 collective-permute-start.10
  70.7 6.0 collective-permute-start.4
  78.7 8.4 fusion.59
  87.1 15.2 %scatter_fusion.1 = f32[16,64,128]{2,1,0:T(8,128)S(1)} fusion(f32[16,64,128]{2,1,0:T(8,128)S(1)} %fusion.59, s32[256]{0:T(256)S(1)} %bitcast.167, f32[256]{0:T(256)S(1)} %get-tuple-element.94), kind=kCustom, calls=%fused_computation.1 | custom fusion | flops 256 | bytes 6144 | tf_op jit(solution)/shard_map/scatter-add | solution.py:59
  102.4 3.8 multiply_add_fusion.1
  109.5 6.0 collective-permute-start.12
  118.4 6.0 collective-permute-start.6
  126.4 2.2 fusion.34
  128.7 15.2 %scatter_fusion.2 = f32[16,64,128]{2,1,0:T(8,128)S(1)} fusion(f32[16,64,128]{2,1,0:T(8,128)S(1)} %fusion.34, s32[256]{0:T(256)S(1)} %bitcast.168, f32[256]{0:T(256)S(1)} %get-tuple-element.93), kind=kCustom, calls=%fused_computation.2 | custom fusion | flops 256 | bytes 6144 | tf_op jit(solution)/shard_map/scatter-add | solution.py:59
  143.9 9.8 multiply_add_fusion
  157.0 6.0 collective-permute-start.14
  163.1 2.1 collective-permute-start.15
  166.2 6.0 collective-permute-start.8
  174.2 2.2 fusion.9
  176.4 15.2 %scatter_fusion.3 = f32[16,64,128]{2,1,0:T(8,128)S(1)} fusion(f32[16,64,128]{2,1,0:T(8,128)S(1)} %fusion.9, s32[256]{0:T(256)S(1)} %bitcast.169, f32[256]{0:T(256)S(1)} %get-tuple-element.57), kind=kCustom, calls=%fused_computation.3 | custom fusion | flops 256 | bytes 6144 | tf_op jit(solution)/shard_map/scatter-add | solution.py:59
  191.7 10.4 fusion.87
  202.3 51.7 %reduce-scatter.2.cloned.1.call-done = f32[16,8,128]{2,1,0:T(8,128)} async-done(((f32[16,64,128]{2,1,0:T(8,128)}), f32[16,8,128]{2,1,0:T(8,128)}) %reduce-scatter.2.cloned.1.call-update) | async-done | bytes 65552 | tf_op jit(solution)/shard_map/reduce_scatter | solution.py:98
  255.5 73.4 %all-reduce.9 = (f32[5]{0:T(128)S(1)}, f32[]{:T(128)}) all-reduce(f32[5]{0:T(128)S(1)} %multiply_reduce_fusion, f32[]{:T(128)} %get-tuple-element.55), channel_id=1, replica_groups=mesh['depth'=32,'shot'=8] {'depth','shot'}, use_global_device_ids=true, to_apply=%region_7.8 | all-reduce | flops 6 | bytes 48 | tf_op jit(solution)/shard_map/psum | solution.py:105
  332.0 74.0 %psum.87 = f32[]{:T(128)} all-reduce(f32[]{:T(128)} %fusion.360), channel_id=1, replica_groups=mesh['depth'=32,'shot'=8] {'depth','shot'}, use_global_device_ids=true, to_apply=%region_13.14 | all-reduce | flops 1 | bytes 8 | tf_op jit(solution)/shard_map/psum | solution.py:110
  407.9 74.3 %psum.88 = f32[]{:T(128)} all-reduce(f32[]{:T(128)} %get-tuple-element.53), channel_id=1, replica_groups=mesh['depth'=32,'shot'=8] {'depth','shot'}, use_global_device_ids=true, to_apply=%region_15.16 | all-reduce | flops 1 | bytes 8 | tf_op jit(solution)/shard_map/psum | solution.py:110
  484.0 73.3 %psum.89 = f32[]{:T(128)} all-reduce(f32[]{:T(128)} %get-tuple-element.40), channel_id=1, replica_groups=mesh['depth'=32,'shot'=8] {'depth','shot'}, use_global_device_ids=true, to_apply=%region_17.18 | all-reduce | flops 1 | bytes 8 | tf_op jit(solution)/shard_map/psum | solution.py:110
  559.2 74.3 %all-reduce.8 = (f32[]{:T(128)}, f32[]{:T(128)}) all-reduce(f32[]{:T(128)} %get-tuple-element.51, f32[]{:T(128)} %get-tuple-element.39), channel_id=1, replica_groups=mesh['depth'=32,'shot'=8] {'depth','shot'}, use_global_device_ids=true, to_apply=%region_19.20 | all-reduce | flops 2 | bytes 16 | tf_op jit(solution)/shard_map/psum | solution.py:110
  636.8 73.4 %psum.91 = f32[]{:T(128)} all-reduce(f32[]{:T(128)} %fusion.347), channel_id=1, replica_groups=mesh['depth'=32,'shot'=8] {'depth','shot'}, use_global_device_ids=true, to_apply=%region_21.22 | all-reduce | flops 1 | bytes 8 | tf_op jit(solution)/shard_map/psum | solution.py:116
  712.1 74.2 %psum.92 = f32[]{:T(128)} all-reduce(f32[]{:T(128)} %get-tuple-element.49), channel_id=1, replica_groups=mesh['depth'=32,'shot'=8] {'depth','shot'}, use_global_device_ids=true, to_apply=%region_23.24 | all-reduce | flops 1 | bytes 8 | tf_op jit(solution)/shard_map/psum | solution.py:116
  788.2 73.4 %psum.93 = f32[]{:T(128)} all-reduce(f32[]{:T(128)} %fusion.355), channel_id=1, replica_groups=mesh['depth'=32,'shot'=8] {'depth','shot'}, use_global_device_ids=true, to_apply=%region_25.26 | all-reduce | flops 1 | bytes 8 | tf_op jit(solution)/shard_map/psum | solution.py:116
  863.4 74.2 %psum.94 = f32[]{:T(128)} all-reduce(f32[]{:T(128)} %get-tuple-element.47), channel_id=1, replica_groups=mesh['depth'=32,'shot'=8] {'depth','shot'}, use_global_device_ids=true, to_apply=%region_27.28 | all-reduce | flops 1 | bytes 8 | tf_op jit(solution)/shard_map/psum | solution.py:116
  939.5 73.5 %psum.95 = f32[]{:T(128)} all-reduce(f32[]{:T(128)} %fusion.367), channel_id=1, replica_groups=mesh['depth'=32,'shot'=8] {'depth','shot'}, use_global_device_ids=true, to_apply=%region_29.30 | all-reduce | flops 1 | bytes 8 | tf_op jit(solution)/shard_map/psum | solution.py:116
  1014.9 29.8 %all_gather.3 = f32[16,64,128]{2,1,0:T(8,128)S(1)} all-gather(f32[16,8,128]{2,1,0:T(8,128)S(1)} %get-tuple-element.45), channel_id=1, replica_groups=mesh['depth'=32,'shot'=8] {'shot'}, dimensions={1}, use_global_device_ids=true | all-gather | bytes 589824 | tf_op jit(solution)/shard_map/all_gather | solution.py:126
  (97 shorter events, 39.3 us)
Async XLA Ops:
  7.2 246.8 %reduce-scatter.2.cloned.1.call-start = ((), (), s32[]{:S(2)}) async-start(), calls=%async_computation.1 | async-start | bytes 589824 | tf_op jit(solution)/shard_map/reduce_scatter | solution.py:98
  8.9 48.0 %collective-permute-start.2 = (f32[4,64,128]{2,1,0:T(8,128)}, f32[4,64,128]{2,1,0:T(8,128)S(1)}, u32[]{:S(2)}, u32[]{:S(2)}) collective-permute-start(f32[4,64,128]{2,1,0:T(8,128)} %get-tuple-element.80), channel_id=1, source_target_pairs={{8,0},{16,8},{24,16},{32,24},{40,32},{48,40},{56,48},{64,56},{72,6... | collective-permute-start | bytes 393224 | tf_op jit(solution)/shard_map/ppermute | solution.py:21
  12.8 11.5 %copy-start.14 = (f32[1,4,256]{2,1,0:T(4,128)S(1)}, f32[1,4,256]{2,1,0:T(4,128)}, u32[]{:S(2)}) copy-start(f32[1,4,256]{2,1,0:T(4,128)} %param.24) | copy-start | bytes 12292
  12.8 11.5 %copy-start.15 = (s32[1,256]{1,0:T(1,128)S(1)}, s32[1,256]{1,0:T(1,128)}, u32[]{:S(2)}) copy-start(s32[1,256]{1,0:T(1,128)} %param.23) | copy-start | bytes 3076
  12.8 12.1 %copy-start.13 = (f32[1,4]{1,0:T(1,128)S(1)}, f32[1,4]{1,0:T(1,128)}, u32[]{:S(2)}) copy-start(f32[1,4]{1,0:T(1,128)} %param.22) | copy-start | bytes 52
  12.9 44.1 %collective-permute-start.3 = (f32[4,64,128]{2,1,0:T(8,128)S(1)}, f32[4,64,128]{2,1,0:T(8,128)S(1)}, u32[]{:S(2)}, u32[]{:S(2)}) collective-permute-start(f32[4,64,128]{2,1,0:T(8,128)S(1)} %get-tuple-element.81), channel_id=1, source_target_pairs={{0,8},{8,16},{16,24},{24,32},{32,40},{40,48},{48,56},{56,64},{64,7... | collective-permute-start | bytes 393224 | tf_op jit(solution)/shard_map/ppermute | solution.py:19
  14.9 16.1 %copy-start.12 = (f32[1,16,64,128]{3,2,1,0:T(8,128)S(1)}, f32[1,16,64,128]{3,2,1,0:T(8,128)}, u32[]{:S(2)}) copy-start(f32[1,16,64,128]{3,2,1,0:T(8,128)} %param.19) | copy-start | bytes 1572868
  16.1 12.1 %copy-start.16 = (s32[3]{0:T(128)S(1)}, s32[3]{0:T(128)}, u32[]{:S(2)}) copy-start(s32[3]{0:T(128)} %constant.251.clone.1) | copy-start | bytes 40
  16.1 14.9 %copy-start.3 = (f32[1,16,64,128]{3,2,1,0:T(8,128)S(1)}, f32[1,16,64,128]{3,2,1,0:T(8,128)}, u32[]{:S(2)}) copy-start(f32[1,16,64,128]{3,2,1,0:T(8,128)} %param.20) | copy-start | bytes 1572868
  16.2 12.8 %collective-permute-start = (f32[4,64,128]{2,1,0:T(8,128)S(1)}, f32[4,64,128]{2,1,0:T(8,128)S(1)}, u32[]{:S(2)}, u32[]{:S(2)}) collective-permute-start(f32[4,64,128]{2,1,0:T(8,128)S(1)} %get-tuple-element.82), channel_id=1, source_target_pairs={{8,0},{16,8},{24,16},{32,24},{40,32},{48,40},{56,48},{64,56},{72,6... | collective-permute-start | bytes 393224 | tf_op jit(solution)/shard_map/ppermute | solution.py:21
  22.3 8.7 collective-permute-start.1
  33.0 24.0 %copy-start.2 = (f32[1,16,64,128]{3,2,1,0:T(8,128)S(1)}, f32[1,16,64,128]{3,2,1,0:T(8,128)}, u32[]{:S(2)}) copy-start(f32[1,16,64,128]{3,2,1,0:T(8,128)} %param.18) | copy-start | bytes 1572868
  60.6 18.1 %copy-start.8 = (f32[16,64,128]{2,1,0:T(8,128)}, f32[16,64,128]{2,1,0:T(8,128)S(1)}, u32[]{:S(2)}) copy-start(f32[16,64,128]{2,1,0:T(8,128)S(1)} %get-tuple-element.73) | copy-start | bytes 1572868
  61.3 17.4 %collective-permute-start.10 = (f32[4,64,128]{2,1,0:T(8,128)}, f32[4,64,128]{2,1,0:T(8,128)S(1)}, u32[]{:S(2)}, u32[]{:S(2)}) collective-permute-start(f32[4,64,128]{2,1,0:T(8,128)} %get-tuple-element.71), channel_id=1, source_target_pairs={{8,0},{16,8},{24,16},{32,24},{40,32},{48,40},{56,48},{64,56},{72,6... | collective-permute-start | bytes 393224 | tf_op jit(solution)/shard_map/ppermute | solution.py:21
  65.4 13.3 %collective-permute-start.11 = (f32[4,64,128]{2,1,0:T(8,128)S(1)}, f32[4,64,128]{2,1,0:T(8,128)S(1)}, u32[]{:S(2)}, u32[]{:S(2)}) collective-permute-start(f32[4,64,128]{2,1,0:T(8,128)S(1)} %get-tuple-element.72), channel_id=1, source_target_pairs={{0,8},{8,16},{16,24},{24,32},{32,40},{40,48},{48,56},{56,64},{64,7... | collective-permute-start | bytes 393224 | tf_op jit(solution)/shard_map/ppermute | solution.py:19
  70.7 31.6 %collective-permute-start.4 = (f32[4,64,128]{2,1,0:T(8,128)}, f32[4,64,128]{2,1,0:T(8,128)}, u32[]{:S(2)}, u32[]{:S(2)}) collective-permute-start(f32[4,64,128]{2,1,0:T(8,128)} %get-tuple-element.78), channel_id=1, source_target_pairs={{8,0},{16,8},{24,16},{32,24},{40,32},{48,40},{56,48},{64,56},{72,6... | collective-permute-start | bytes 393224 | tf_op jit(solution)/shard_map/ppermute | solution.py:21
  76.8 25.6 %collective-permute-start.5 = (f32[4,64,128]{2,1,0:T(8,128)}, f32[4,64,128]{2,1,0:T(8,128)}, u32[]{:S(2)}, u32[]{:S(2)}) collective-permute-start(f32[4,64,128]{2,1,0:T(8,128)} %get-tuple-element.79), channel_id=1, source_target_pairs={{0,8},{8,16},{16,24},{24,32},{32,40},{40,48},{48,56},{56,64},{64,7... | collective-permute-start | bytes 393224 | tf_op jit(solution)/shard_map/ppermute | solution.py:19
  106.2 9.4 copy-start.9
  109.5 16.9 %collective-permute-start.12 = (f32[4,64,128]{2,1,0:T(8,128)}, f32[4,64,128]{2,1,0:T(8,128)S(1)}, u32[]{:S(2)}, u32[]{:S(2)}) collective-permute-start(f32[4,64,128]{2,1,0:T(8,128)} %get-tuple-element.68), channel_id=1, source_target_pairs={{8,0},{16,8},{24,16},{32,24},{40,32},{48,40},{56,48},{64,56},{72,6... | collective-permute-start | bytes 393224 | tf_op jit(solution)/shard_map/ppermute | solution.py:21
  115.6 10.8 %collective-permute-start.13 = (f32[4,64,128]{2,1,0:T(8,128)}, f32[4,64,128]{2,1,0:T(8,128)}, u32[]{:S(2)}, u32[]{:S(2)}) collective-permute-start(f32[4,64,128]{2,1,0:T(8,128)} %get-tuple-element.69), channel_id=1, source_target_pairs={{0,8},{8,16},{16,24},{24,32},{32,40},{40,48},{48,56},{56,64},{64,7... | collective-permute-start | bytes 393224 | tf_op jit(solution)/shard_map/ppermute | solution.py:19
  117.5 8.9 copy-start.10
  118.4 25.5 %collective-permute-start.6 = (f32[4,64,128]{2,1,0:T(8,128)}, f32[4,64,128]{2,1,0:T(8,128)S(1)}, u32[]{:S(2)}, u32[]{:S(2)}) collective-permute-start(f32[4,64,128]{2,1,0:T(8,128)} %get-tuple-element.76), channel_id=1, source_target_pairs={{8,0},{16,8},{24,16},{32,24},{40,32},{48,40},{56,48},{64,56},{72,6... | collective-permute-start | bytes 393224 | tf_op jit(solution)/shard_map/ppermute | solution.py:21
  124.5 19.4 %collective-permute-start.7 = (f32[4,64,128]{2,1,0:T(8,128)}, f32[4,64,128]{2,1,0:T(8,128)S(1)}, u32[]{:S(2)}, u32[]{:S(2)}) collective-permute-start(f32[4,64,128]{2,1,0:T(8,128)} %get-tuple-element.77), channel_id=1, source_target_pairs={{0,8},{8,16},{16,24},{24,32},{32,40},{40,48},{48,56},{56,64},{64,7... | collective-permute-start | bytes 393224 | tf_op jit(solution)/shard_map/ppermute | solution.py:19
  153.7 9.4 copy-start.6
  157.0 17.1 %collective-permute-start.14 = (f32[4,64,128]{2,1,0:T(8,128)}, f32[4,64,128]{2,1,0:T(8,128)S(1)}, u32[]{:S(2)}, u32[]{:S(2)}) collective-permute-start(f32[4,64,128]{2,1,0:T(8,128)} %get-tuple-element.65), channel_id=1, source_target_pairs={{8,0},{16,8},{24,16},{32,24},{40,32},{48,40},{56,48},{64,56},{72,6... | collective-permute-start | bytes 393224 | tf_op jit(solution)/shard_map/ppermute | solution.py:21
  163.1 11.1 %collective-permute-start.15 = (f32[4,64,128]{2,1,0:T(8,128)}, f32[4,64,128]{2,1,0:T(8,128)}, u32[]{:S(2)}, u32[]{:S(2)}) collective-permute-start(f32[4,64,128]{2,1,0:T(8,128)} %get-tuple-element.66), channel_id=1, source_target_pairs={{0,8},{8,16},{16,24},{24,32},{32,40},{40,48},{48,56},{56,64},{64,7... | collective-permute-start | bytes 393224 | tf_op jit(solution)/shard_map/ppermute | solution.py:19
  165.2 9.0 copy-start.7
  165.4 8.8 copy-start.4
  166.2 25.5 %collective-permute-start.8 = (f32[4,64,128]{2,1,0:T(8,128)}, f32[4,64,128]{2,1,0:T(8,128)S(1)}, u32[]{:S(2)}, u32[]{:S(2)}) collective-permute-start(f32[4,64,128]{2,1,0:T(8,128)} %get-tuple-element.74), channel_id=1, source_target_pairs={{8,0},{16,8},{24,16},{32,24},{40,32},{48,40},{56,48},{64,56},{72,6... | collective-permute-start | bytes 393224 | tf_op jit(solution)/shard_map/ppermute | solution.py:21
  172.2 19.4 %collective-permute-start.9 = (f32[4,64,128]{2,1,0:T(8,128)}, f32[4,64,128]{2,1,0:T(8,128)S(1)}, u32[]{:S(2)}, u32[]{:S(2)}) collective-permute-start(f32[4,64,128]{2,1,0:T(8,128)} %get-tuple-element.75), channel_id=1, source_target_pairs={{0,8},{8,16},{16,24},{24,32},{32,40},{40,48},{48,56},{56,64},{64,7... | collective-permute-start | bytes 393224 | tf_op jit(solution)/shard_map/ppermute | solution.py:19
  191.7 10.5 copy-start.1
  255.5 381.3 %copy-start.11 = (f32[16,8,128]{2,1,0:T(8,128)}, f32[16,8,128]{2,1,0:T(8,128)S(1)}, u32[]{:S(2)}) copy-start(f32[16,8,128]{2,1,0:T(8,128)S(1)} %get-tuple-element.102) | copy-start | bytes 196612
  (2 other events, 16.5 us)
Sparse Core Ops, SparseCore 0:
  202.3 51.6 reduce-scatter.1
where the time goes:
time: 1060 us; the launch traced here: 1050 us
  blocking collectives  768 us (72%)
  other arithmetic  122 us (12%)
  starting transfers between devices  60 us (6%)
  waiting for transfers between devices  53.8 us (5%)
  between operations  37.1 us (4%)
  local copies, waits for them, and re-layouts  11.3 us (1%)
    psum x5, blocking collectives, per_device(): lax.psum(jnp.sum(changes[number] * scaled), ('depth', 'shot'))  369 us
    psum x4, blocking collectives, per_device(): lax.psum(jnp.sum(displaced[number] * search), ('depth', 'shot'))  296 us
    psum x1, blocking collectives, per_device(): lax.psum((pair_dots, last_square), ('depth', 'shot'))  73.4 us
    scatter-add x4, other arithmetic, inject(): volume.at[row_safe, remainder // volume.shape[2], remainder % volume.shap...  69.6 us
    reduce_scatter x1, waiting for transfers between devices, per_device(): lax.psum_scatter(summed, 'shot', scatter_dimension=1, tiled=True)  51.7 us
    ppermute x8, starting transfers between devices, with_halo(): lax.ppermute(head, axis, [((i + 1) % count, i) for i in range(ends)])  44.3 us
    all_gather x1, blocking collectives, per_device(): courant_next = lax.all_gather(next_piece, 'shot', axis=1, tiled=True)  29.8 us
  transfers between devices with their start and end apart: 17, of which 2 were waited for; matrix products, arithmetic and copies ran while one was open for 9% of the time, Pallas kernels for 0%

commit v1 on v0

--- a/solution.py
+++ b/solution.py
@@ -102,7 +102,7 @@
     changes = history[1]
     pair_dots = jnp.sum(displaced * changes, axis=(1, 2, 3))
     last_square = jnp.sum(changes[PAIRS - 1] * changes[PAIRS - 1])
-    curvature, last_square = lax.psum((pair_dots, last_square), ("depth", "shot"))
+    curvature, last_square = lax.psum(lax.psum((pair_dots, last_square), "shot"), "depth")
     inverse = 1.0 / curvature
     search = grad_piece
     alphas = [None] * PAIRS

time: 1060 us -> 1180 us (1.11)
  blocking collectives: 768 us -> 946 us
  waiting for transfers between devices: 53.8 us -> 0.06 us
    psum x4 -> x5, blocking collectives: 296 us -> 387 us  [per_device(): lax.psum(jnp.sum(displaced[number] * search), ('depth', 'shot'))]
    psum x1 -> x4, blocking collectives: 73.4 us -> 153 us  [the longest x2 116 us: per_device(): lax.psum(lax.psum((pair_dots, last_square), 'shot'), 'depth')]
    reduce_scatter x1, waiting for transfers between devices: 51.7 us -> 0.01 us  [per_device(): lax.psum_scatter(summed, 'shot', scatter_dimension=1, tiled=True)]
  transfers between devices with their start and end apart: 17 -> 17, of which waited for: 2 -> 0; matrix products, arithmetic and copies ran while one was open for 9% -> 8% of each run, Pallas kernels for 0% -> 0%
where the time goes in v1:
time: 1180 us; the launch traced here: 1170 us
  blocking collectives  946 us (80%)
  other arithmetic  120 us (10%)
  starting transfers between devices  61.9 us (5%)
  between operations  37.2 us (3%)
    psum x5, blocking collectives, per_device(): lax.psum(jnp.sum(displaced[number] * search), ('depth', 'shot'))  387 us
    psum x5, blocking collectives, per_device(): lax.psum(jnp.sum(changes[number] * scaled), ('depth', 'shot'))  376 us
    psum x2, blocking collectives, per_device(): lax.psum(lax.psum((pair_dots, last_square), 'shot'), 'depth')  116 us
    scatter-add x4, other arithmetic, inject(): volume.at[row_safe, remainder // volume.shape[2], remainder % volume.shap...  69.6 us
    ppermute x8, starting transfers between devices, with_halo(): lax.ppermute(head, axis, [((i + 1) % count, i) for i in range(ends)])  46.4 us
    psum x2, blocking collectives, per_device(): lax.psum((pair_dots, last_square), 'shot')  37.1 us
    all_gather x1, blocking collectives, per_device(): courant_next = lax.all_gather(next_piece, 'shot', axis=1, tiled=True)  29.9 us
  transfers between devices with their start and end apart: 17, of which 0 were waited for; matrix products, arithmetic and copies ran while one was open for 8% of the time, Pallas kernels for 0%

profile of v1, /device:TPU:32, one launch (start us, length us, event | category | flops | bytes accessed | tf_op | source)
XLA Modules:
  0.0 1172.7 jit_solution(16783708896906228173)
XLA Ops:
  8.6 4.0 collective-permute-start
  14.7 6.0 collective-permute-start.2
  29.3 23.9 %scatter_fusion = f32[16,64,128]{2,1,0:T(8,128)S(1)} fusion(f32[16,64,128]{2,1,0:T(8,128)S(1)} %fusion.184, s32[256]{0:T(256)S(1)} %bitcast.166, f32[256]{0:T(256)} %get-tuple-element.91), kind=kCustom, calls=%fused_computation | custom fusion | flops 256 | bytes 6144 | tf_op jit(solution)/shard_map/scatter-add | solution.py:59
  53.3 3.7 fusion.344
  59.8 6.1 collective-permute-start.10
  68.5 6.0 collective-permute-start.4
  76.5 8.4 fusion.59
  84.8 15.2 %scatter_fusion.1 = f32[16,64,128]{2,1,0:T(8,128)S(1)} fusion(f32[16,64,128]{2,1,0:T(8,128)S(1)} %fusion.59, s32[256]{0:T(256)S(1)} %bitcast.167, f32[256]{0:T(256)S(1)} %get-tuple-element.90), kind=kCustom, calls=%fused_computation.1 | custom fusion | flops 256 | bytes 6144 | tf_op jit(solution)/shard_map/scatter-add | solution.py:59
  100.1 2.7 multiply_add_fusion.1
  102.8 6.1 collective-permute-start.12
  114.3 6.0 collective-permute-start.6
  124.2 15.2 %scatter_fusion.2 = f32[16,64,128]{2,1,0:T(8,128)S(1)} fusion(f32[16,64,128]{2,1,0:T(8,128)S(1)} %fusion.34, s32[256]{0:T(256)S(1)} %bitcast.168, f32[256]{0:T(256)S(1)} %get-tuple-element.89), kind=kCustom, calls=%fused_computation.2 | custom fusion | flops 256 | bytes 6144 | tf_op jit(solution)/shard_map/scatter-add | solution.py:59
  139.5 9.0 multiply_add_fusion
  148.5 6.1 collective-permute-start.14
  160.1 6.0 collective-permute-start.8
  170.3 15.2 %scatter_fusion.3 = f32[16,64,128]{2,1,0:T(8,128)S(1)} fusion(f32[16,64,128]{2,1,0:T(8,128)S(1)} %fusion.9, s32[256]{0:T(256)S(1)} %bitcast.169, f32[256]{0:T(256)S(1)} %get-tuple-element.53), kind=kCustom, calls=%fused_computation.3 | custom fusion | flops 256 | bytes 6144 | tf_op jit(solution)/shard_map/scatter-add | solution.py:59
  185.6 10.3 fusion.87
  196.1 19.0 %psum.98 = f32[5]{0:T(128)S(1)} all-reduce(f32[5]{0:T(128)S(1)} %multiply_reduce_fusion), channel_id=1, replica_groups=mesh['depth'=32,'shot'=8] {'shot'}, use_global_device_ids=true, to_apply=%region_7.8 | all-reduce | flops 5 | bytes 40 | tf_op jit(solution)/shard_map/psum | solution.py:105
  215.1 57.0 %psum.99 = f32[5]{0:T(128)S(1)} all-reduce(f32[5]{0:T(128)S(1)} %psum.98), channel_id=1, replica_groups=mesh['depth'=32,'shot'=8] {'depth'}, use_global_device_ids=true, to_apply=%region_8.9 | all-reduce | flops 5 | bytes 40 | tf_op jit(solution)/shard_map/psum | solution.py:105
  274.9 92.4 %psum.102 = f32[]{:T(128)} all-reduce(f32[]{:T(128)} %get-tuple-element.51), channel_id=1, replica_groups=mesh['depth'=32,'shot'=8] {'depth','shot'}, use_global_device_ids=true, to_apply=%region_13.14 | all-reduce | flops 1 | bytes 8 | tf_op jit(solution)/shard_map/psum | solution.py:110
  369.1 73.6 %psum.103 = f32[]{:T(128)} all-reduce(f32[]{:T(128)} %fusion.360), channel_id=1, replica_groups=mesh['depth'=32,'shot'=8] {'depth','shot'}, use_global_device_ids=true, to_apply=%region_15.16 | all-reduce | flops 1 | bytes 8 | tf_op jit(solution)/shard_map/psum | solution.py:110
  444.7 75.4 %psum.104 = f32[]{:T(128)} all-reduce(f32[]{:T(128)} %get-tuple-element.49), channel_id=1, replica_groups=mesh['depth'=32,'shot'=8] {'depth','shot'}, use_global_device_ids=true, to_apply=%region_17.18 | all-reduce | flops 1 | bytes 8 | tf_op jit(solution)/shard_map/psum | solution.py:110
  521.9 73.3 %psum.105 = f32[]{:T(128)} all-reduce(f32[]{:T(128)} %get-tuple-element.40), channel_id=1, replica_groups=mesh['depth'=32,'shot'=8] {'depth','shot'}, use_global_device_ids=true, to_apply=%region_19.20 | all-reduce | flops 1 | bytes 8 | tf_op jit(solution)/shard_map/psum | solution.py:110
  597.2 18.1 %psum.100 = f32[]{:T(128)} all-reduce(f32[]{:T(128)} %get-tuple-element.39), channel_id=1, replica_groups=mesh['depth'=32,'shot'=8] {'shot'}, use_global_device_ids=true, to_apply=%region_10.11 | all-reduce | flops 1 | bytes 8 | tf_op jit(solution)/shard_map/psum | solution.py:105
  615.3 72.0 %psum.106 = f32[]{:T(128)} all-reduce(f32[]{:T(128)} %get-tuple-element.47), channel_id=1, replica_groups=mesh['depth'=32,'shot'=8] {'depth','shot'}, use_global_device_ids=true, to_apply=%region_21.22 | all-reduce | flops 1 | bytes 8 | tf_op jit(solution)/shard_map/psum | solution.py:110
  687.3 59.2 %psum.101 = f32[]{:T(128)} all-reduce(f32[]{:T(128)} %psum.100), channel_id=1, replica_groups=mesh['depth'=32,'shot'=8] {'depth'}, use_global_device_ids=true, to_apply=%region_11.12 | all-reduce | flops 1 | bytes 8 | tf_op jit(solution)/shard_map/psum | solution.py:105
  749.8 82.6 %psum.107 = f32[]{:T(128)} all-reduce(f32[]{:T(128)} %fusion.347), channel_id=1, replica_groups=mesh['depth'=32,'shot'=8] {'depth','shot'}, use_global_device_ids=true, to_apply=%region_23.24 | all-reduce | flops 1 | bytes 8 | tf_op jit(solution)/shard_map/psum | solution.py:116
  834.3 72.1 %psum.108 = f32[]{:T(128)} all-reduce(f32[]{:T(128)} %get-tuple-element.45), channel_id=1, replica_groups=mesh['depth'=32,'shot'=8] {'depth','shot'}, use_global_device_ids=true, to_apply=%region_25.26 | all-reduce | flops 1 | bytes 8 | tf_op jit(solution)/shard_map/psum | solution.py:116
  908.3 73.9 %psum.109 = f32[]{:T(128)} all-reduce(f32[]{:T(128)} %fusion.355), channel_id=1, replica_groups=mesh['depth'=32,'shot'=8] {'depth','shot'}, use_global_device_ids=true, to_apply=%region_27.28 | all-reduce | flops 1 | bytes 8 | tf_op jit(solution)/shard_map/psum | solution.py:116
  984.0 73.2 %psum.110 = f32[]{:T(128)} all-reduce(f32[]{:T(128)} %get-tuple-element.43), channel_id=1, replica_groups=mesh['depth'=32,'shot'=8] {'depth','shot'}, use_global_device_ids=true, to_apply=%region_29.30 | all-reduce | flops 1 | bytes 8 | tf_op jit(solution)/shard_map/psum | solution.py:116
  1059.2 74.1 %psum.111 = f32[]{:T(128)} all-reduce(f32[]{:T(128)} %fusion.367), channel_id=1, replica_groups=mesh['depth'=32,'shot'=8] {'depth','shot'}, use_global_device_ids=true, to_apply=%region_31.32 | all-reduce | flops 1 | bytes 8 | tf_op jit(solution)/shard_map/psum | solution.py:116
  1135.2 29.9 %all_gather.3 = f32[16,64,128]{2,1,0:T(8,128)S(1)} all-gather(f32[16,8,128]{2,1,0:T(8,128)S(1)} %get-tuple-element.41), channel_id=1, replica_groups=mesh['depth'=32,'shot'=8] {'shot'}, dimensions={1}, use_global_device_ids=true | all-gather | bytes 589824 | tf_op jit(solution)/shard_map/all_gather | solution.py:126
  (101 shorter events, 39.6 us)
Async XLA Ops:
  7.2 266.2 %reduce-scatter.2.cloned.1.call-start = ((), (), s32[]{:S(2)}) async-start(), calls=%async_computation.1 | async-start | bytes 589824 | tf_op jit(solution)/shard_map/reduce_scatter | solution.py:98
  7.2 20.1 %copy-start.12 = (f32[1,16,64,128]{3,2,1,0:T(8,128)S(1)}, f32[1,16,64,128]{3,2,1,0:T(8,128)}, u32[]{:S(2)}) copy-start(f32[1,16,64,128]{3,2,1,0:T(8,128)} %param.19) | copy-start | bytes 1572868
  8.5 14.1 %copy-start.14 = (f32[1,4,256]{2,1,0:T(4,128)S(1)}, f32[1,4,256]{2,1,0:T(4,128)}, u32[]{:S(2)}) copy-start(f32[1,4,256]{2,1,0:T(4,128)} %param.24) | copy-start | bytes 12292
  8.6 14.1 %copy-start.15 = (s32[1,256]{1,0:T(1,128)S(1)}, s32[1,256]{1,0:T(1,128)}, u32[]{:S(2)}) copy-start(s32[1,256]{1,0:T(1,128)} %param.23) | copy-start | bytes 3076
  8.6 14.7 %copy-start.13 = (f32[1,4]{1,0:T(1,128)S(1)}, f32[1,4]{1,0:T(1,128)}, u32[]{:S(2)}) copy-start(f32[1,4]{1,0:T(1,128)} %param.22) | copy-start | bytes 52
  8.6 18.0 %copy-start.16 = (s32[3]{0:T(128)S(1)}, s32[3]{0:T(128)}, u32[]{:S(2)}) copy-start(s32[3]{0:T(128)} %constant.251.clone.1) | copy-start | bytes 40
  8.6 18.7 %copy-start.3 = (f32[1,16,64,128]{3,2,1,0:T(8,128)S(1)}, f32[1,16,64,128]{3,2,1,0:T(8,128)}, u32[]{:S(2)}) copy-start(f32[1,16,64,128]{3,2,1,0:T(8,128)} %param.20) | copy-start | bytes 1572868
  8.6 18.7 %collective-permute-start = (f32[4,64,128]{2,1,0:T(8,128)S(1)}, f32[4,64,128]{2,1,0:T(8,128)S(1)}, u32[]{:S(2)}, u32[]{:S(2)}) collective-permute-start(f32[4,64,128]{2,1,0:T(8,128)S(1)} %get-tuple-element.78), channel_id=1, source_target_pairs={{8,0},{16,8},{24,16},{32,24},{40,32},{48,40},{56,48},{64,56},{72,6... | collective-permute-start | bytes 393224 | tf_op jit(solution)/shard_map/ppermute | solution.py:21
  12.7 14.6 %collective-permute-start.1 = (f32[4,64,128]{2,1,0:T(8,128)S(1)}, f32[4,64,128]{2,1,0:T(8,128)S(1)}, u32[]{:S(2)}, u32[]{:S(2)}) collective-permute-start(f32[4,64,128]{2,1,0:T(8,128)S(1)} %get-tuple-element.79), channel_id=1, source_target_pairs={{0,8},{8,16},{16,24},{24,32},{32,40},{40,48},{48,56},{56,64},{64,7... | collective-permute-start | bytes 393224 | tf_op jit(solution)/shard_map/ppermute | solution.py:19
  14.7 38.6 %collective-permute-start.2 = (f32[4,64,128]{2,1,0:T(8,128)S(1)}, f32[4,64,128]{2,1,0:T(8,128)S(1)}, u32[]{:S(2)}, u32[]{:S(2)}) collective-permute-start(f32[4,64,128]{2,1,0:T(8,128)S(1)} %get-tuple-element.76), channel_id=1, source_target_pairs={{8,0},{16,8},{24,16},{32,24},{40,32},{48,40},{56,48},{64,56},{72,6... | collective-permute-start | bytes 393224 | tf_op jit(solution)/shard_map/ppermute | solution.py:21
  20.7 32.6 %collective-permute-start.3 = (f32[4,64,128]{2,1,0:T(8,128)S(1)}, f32[4,64,128]{2,1,0:T(8,128)S(1)}, u32[]{:S(2)}, u32[]{:S(2)}) collective-permute-start(f32[4,64,128]{2,1,0:T(8,128)S(1)} %get-tuple-element.77), channel_id=1, source_target_pairs={{0,8},{8,16},{16,24},{24,32},{32,40},{40,48},{48,56},{56,64},{64,7... | collective-permute-start | bytes 393224 | tf_op jit(solution)/shard_map/ppermute | solution.py:19
  29.3 24.0 %copy-start = (f32[16,64,128]{2,1,0:T(8,128)S(1)}, f32[16,64,128]{2,1,0:T(8,128)}, u32[]{:S(2)}) copy-start(f32[16,64,128]{2,1,0:T(8,128)} %param.16) | copy-start | bytes 1572868
  57.0 19.5 %copy-start.8 = (f32[16,64,128]{2,1,0:T(8,128)}, f32[16,64,128]{2,1,0:T(8,128)S(1)}, u32[]{:S(2)}) copy-start(f32[16,64,128]{2,1,0:T(8,128)S(1)} %get-tuple-element.69) | copy-start | bytes 1572868
  59.8 16.6 %collective-permute-start.10 = (f32[4,64,128]{2,1,0:T(8,128)S(1)}, f32[4,64,128]{2,1,0:T(8,128)S(1)}, u32[]{:S(2)}, u32[]{:S(2)}) collective-permute-start(f32[4,64,128]{2,1,0:T(8,128)S(1)} %get-tuple-element.67), channel_id=1, source_target_pairs={{8,0},{16,8},{24,16},{32,24},{40,32},{48,40},{56,48},{64,56},{72,6... | collective-permute-start | bytes 393224 | tf_op jit(solution)/shard_map/ppermute | solution.py:21
  65.9 10.6 collective-permute-start.11
  68.5 31.6 %collective-permute-start.4 = (f32[4,64,128]{2,1,0:T(8,128)}, f32[4,64,128]{2,1,0:T(8,128)S(1)}, u32[]{:S(2)}, u32[]{:S(2)}) collective-permute-start(f32[4,64,128]{2,1,0:T(8,128)} %get-tuple-element.74), channel_id=1, source_target_pairs={{8,0},{16,8},{24,16},{32,24},{40,32},{48,40},{56,48},{64,56},{72,6... | collective-permute-start | bytes 393224 | tf_op jit(solution)/shard_map/ppermute | solution.py:21
  74.5 25.6 %collective-permute-start.5 = (f32[4,64,128]{2,1,0:T(8,128)S(1)}, f32[4,64,128]{2,1,0:T(8,128)S(1)}, u32[]{:S(2)}, u32[]{:S(2)}) collective-permute-start(f32[4,64,128]{2,1,0:T(8,128)S(1)} %get-tuple-element.75), channel_id=1, source_target_pairs={{0,8},{8,16},{16,24},{24,32},{32,40},{40,48},{48,56},{56,64},{64,7... | collective-permute-start | bytes 393224 | tf_op jit(solution)/shard_map/ppermute | solution.py:19
  102.8 9.3 copy-start.9
  102.8 19.4 %collective-permute-start.12 = (f32[4,64,128]{2,1,0:T(8,128)S(1)}, f32[4,64,128]{2,1,0:T(8,128)S(1)}, u32[]{:S(2)}, u32[]{:S(2)}) collective-permute-start(f32[4,64,128]{2,1,0:T(8,128)S(1)} %get-tuple-element.64), channel_id=1, source_target_pairs={{8,0},{16,8},{24,16},{32,24},{40,32},{48,40},{56,48},{64,56},{72,6... | collective-permute-start | bytes 393224 | tf_op jit(solution)/shard_map/ppermute | solution.py:21
  108.9 13.4 %collective-permute-start.13 = (f32[4,64,128]{2,1,0:T(8,128)S(1)}, f32[4,64,128]{2,1,0:T(8,128)S(1)}, u32[]{:S(2)}, u32[]{:S(2)}) collective-permute-start(f32[4,64,128]{2,1,0:T(8,128)S(1)} %get-tuple-element.65), channel_id=1, source_target_pairs={{0,8},{8,16},{16,24},{24,32},{32,40},{40,48},{48,56},{56,64},{64,7... | collective-permute-start | bytes 393224 | tf_op jit(solution)/shard_map/ppermute | solution.py:19
  113.5 25.9 %copy-start.5 = (f32[16,64,128]{2,1,0:T(8,128)}, f32[16,64,128]{2,1,0:T(8,128)S(1)}, u32[]{:S(2)}) copy-start(f32[16,64,128]{2,1,0:T(8,128)S(1)} %scatter-add.45) | copy-start | bytes 1572868
  114.3 25.2 %collective-permute-start.6 = (f32[4,64,128]{2,1,0:T(8,128)}, f32[4,64,128]{2,1,0:T(8,128)S(1)}, u32[]{:S(2)}, u32[]{:S(2)}) collective-permute-start(f32[4,64,128]{2,1,0:T(8,128)} %get-tuple-element.72), channel_id=1, source_target_pairs={{8,0},{16,8},{24,16},{32,24},{40,32},{48,40},{56,48},{64,56},{72,6... | collective-permute-start | bytes 393224 | tf_op jit(solution)/shard_map/ppermute | solution.py:21
  120.3 19.2 %collective-permute-start.7 = (f32[4,64,128]{2,1,0:T(8,128)}, f32[4,64,128]{2,1,0:T(8,128)}, u32[]{:S(2)}, u32[]{:S(2)}) collective-permute-start(f32[4,64,128]{2,1,0:T(8,128)} %get-tuple-element.73), channel_id=1, source_target_pairs={{0,8},{8,16},{16,24},{24,32},{32,40},{40,48},{48,56},{56,64},{64,7... | collective-permute-start | bytes 393224 | tf_op jit(solution)/shard_map/ppermute | solution.py:19
  148.5 9.5 copy-start.6
  148.5 19.6 %collective-permute-start.14 = (f32[4,64,128]{2,1,0:T(8,128)S(1)}, f32[4,64,128]{2,1,0:T(8,128)S(1)}, u32[]{:S(2)}, u32[]{:S(2)}) collective-permute-start(f32[4,64,128]{2,1,0:T(8,128)S(1)} %get-tuple-element.61), channel_id=1, source_target_pairs={{8,0},{16,8},{24,16},{32,24},{40,32},{48,40},{56,48},{64,56},{72,6... | collective-permute-start | bytes 393224 | tf_op jit(solution)/shard_map/ppermute | solution.py:21
  154.5 13.5 %collective-permute-start.15 = (f32[4,64,128]{2,1,0:T(8,128)S(1)}, f32[4,64,128]{2,1,0:T(8,128)}, u32[]{:S(2)}, u32[]{:S(2)}) collective-permute-start(f32[4,64,128]{2,1,0:T(8,128)S(1)} %get-tuple-element.62), channel_id=1, source_target_pairs={{0,8},{8,16},{16,24},{24,32},{32,40},{40,48},{48,56},{56,64},{64,7... | collective-permute-start | bytes 393224 | tf_op jit(solution)/shard_map/ppermute | solution.py:19
  159.4 26.2 %copy-start.4 = (f32[16,64,128]{2,1,0:T(8,128)}, f32[16,64,128]{2,1,0:T(8,128)S(1)}, u32[]{:S(2)}) copy-start(f32[16,64,128]{2,1,0:T(8,128)S(1)} %scatter-add.46) | copy-start | bytes 1572868
  159.4 8.7 copy-start.7
  160.1 25.5 %collective-permute-start.8 = (f32[4,64,128]{2,1,0:T(8,128)}, f32[4,64,128]{2,1,0:T(8,128)S(1)}, u32[]{:S(2)}, u32[]{:S(2)}) collective-permute-start(f32[4,64,128]{2,1,0:T(8,128)} %get-tuple-element.70), channel_id=1, source_target_pairs={{8,0},{16,8},{24,16},{32,24},{40,32},{48,40},{56,48},{64,56},{72,6... | collective-permute-start | bytes 393224 | tf_op jit(solution)/shard_map/ppermute | solution.py:21
  166.2 19.4 %collective-permute-start.9 = (f32[4,64,128]{2,1,0:T(8,128)}, f32[4,64,128]{2,1,0:T(8,128)S(1)}, u32[]{:S(2)}, u32[]{:S(2)}) collective-permute-start(f32[4,64,128]{2,1,0:T(8,128)} %get-tuple-element.71), channel_id=1, source_target_pairs={{0,8},{8,16},{16,24},{24,32},{32,40},{40,48},{48,56},{56,64},{64,7... | collective-permute-start | bytes 393224 | tf_op jit(solution)/shard_map/ppermute | solution.py:19
  185.6 10.4 copy-start.1
  274.9 474.9 %copy-start.11 = (f32[16,8,128]{2,1,0:T(8,128)}, f32[16,8,128]{2,1,0:T(8,128)S(1)}, u32[]{:S(2)}) copy-start(f32[16,8,128]{2,1,0:T(8,128)S(1)} %get-tuple-element.98) | copy-start | bytes 196612
  (2 other events, 14.8 us)
Sparse Core Ops, SparseCore 0:
  196.1 51.9 reduce-scatter.1
